TPU v7x, 32 devices: a whole 2x2x4 slice. The times are simulated.
32 devices in a mesh: seq: 8 (over z, x), exp: 4 (over y, core).
Axes of the slice: x: 2, y: 2, z: 4, core: 2. Of those that a mesh axis runs over, the one named last changes fastest.
Arguments:
- block_input: float32 [4096, 768], P(('seq', 'exp')), may hold values from -6 to 6
- seq_lengths: int32 [10], replicated, may hold values from 1 to 2048, 4096 in all
- expert_ids: int32 [4096, 1], P(('seq', 'exp')), may hold values from 0 to 3
- output_grad: float32 [4096, 768], P(('seq', 'exp')), may hold values from -6 to 6
- mixer_gain: float32 [768], replicated, may hold values from 0.5 to 1.5
- in_proj: float32 [768, 3072], replicated, may hold values from -0.21875 to 0.21875
- conv_weight: float32 [4, 1536], replicated, may hold values from -3 to 3
- conv_bias: float32 [1536], replicated, may hold values from -1.75 to 1.75
- state_proj: float32 [1536, 80], replicated, may hold values from -0.15625 to 0.15625
- step_proj: float32 [48, 1536], replicated, may hold values from -0.875 to 0.875
- step_bias: float32 [1536], replicated, may hold values from -7 to -2.5
- decay_log: float32 [1536, 16], replicated, may hold values from 0 to 2.77
- skip_gain: float32 [1536], replicated, may hold values from 0.5 to 1.5
- out_proj: float32 [1536, 768], replicated, may hold values from -0.3125 to 0.3125
- router_gain: float32 [768], replicated, may hold values from 0.5 to 1.5
- router: float32 [768, 4], replicated, may hold values from -0.15625 to 0.15625
- expert_up: float32 [4, 768, 3072], P('exp', None, 'seq'), may hold values from -0.21875 to 0.21875
- expert_down: float32 [4, 3072, 768], P('exp', 'seq'), may hold values from -0.875 to 0.875
Outputs:
- block_output: float32 [4096, 768], P(('seq', 'exp'))
- input_grad: float32 [4096, 768], P(('seq', 'exp'))
- grad_mixer_gain: float32 [768], replicated
- grad_in_proj: float32 [768, 3072], replicated
- grad_conv_weight: float32 [4, 1536], replicated
- grad_conv_bias: float32 [1536], replicated
- grad_state_proj: float32 [1536, 80], replicated
- grad_step_proj: float32 [48, 1536], replicated
- grad_step_bias: float32 [1536], replicated
- grad_decay_log: float32 [1536, 16], replicated
- grad_skip_gain: float32 [1536], replicated
- grad_out_proj: float32 [1536, 768], replicated
- grad_router_gain: float32 [768], replicated
- grad_router: float32 [768, 4], replicated
- grad_expert_up: float32 [4, 768, 3072], P('exp', None, 'seq')
- grad_expert_down: float32 [4, 3072, 768], P('exp', 'seq')
- expert_load: int32 [4], replicated
- dropped_load: int32 [4], replicated
All inputs are finite; a program needn't handle non-finite values.
Results may differ from a plain program's by a relative error of at most 0.0003.
Values sent between devices are 32-bit elements; how exact they have to be, the bound alone decides.
No kernel may reach another device: no remote copies, remote signals or barrier semaphores. Data moves between devices by JAX's collectives and lax.ppermute only.
A program may use at most 448 MiB of HBM per device.

v0:
```python
import jax
import jax.numpy as jnp
from jax import lax
from jax.sharding import PartitionSpec as P

precise = lax.Precision.HIGHEST
epsilon = 1e-05


def passed_along(block, axis, distance):
    devices = range(lax.axis_size(axis))
    route = [(i - distance, i) for i in devices if i - distance in devices]
    return lax.ppermute(block, axis, route)


def entering(value, axis, join, neutral, backward):
    count, mine = (lax.axis_size(axis), lax.axis_index(axis))
    pieces = jax.tree.map(lambda part: lax.all_gather(part, axis), value)
    if backward:
        pieces = jax.tree.map(lambda part: part[::-1], pieces)
        mine = count - 1 - mine
    so_far = jax.tree.map(
        lambda part, zero: jnp.full_like(part, 0) + jnp.asarray(zero, part.dtype), value, neutral
    )

    def lap(position, so_far):
        longer = join(so_far, jax.tree.map(lambda part: part[position], pieces))
        return jax.tree.map(lambda new, old: jnp.where(position < mine, new, old), longer, so_far)

    return lax.fori_loop(0, count - 1, lap, so_far)


def matmul_high(left, right):
    return jnp.dot(left, right, precision=precise, preferred_element_type=jnp.float32)


def rms_scale(values_in, gain):
    return (
        values_in
        * lax.rsqrt(jnp.mean(values_in * values_in, axis=1, keepdims=True) + epsilon)
        * gain
    )


def chain_states(earlier, later):
    return (later[0] * earlier[0], later[0] * earlier[1] + later[1])


def per_device(
    block_input,
    seq_lengths,
    expert_ids,
    output_grad,
    mixer_gain,
    in_proj,
    conv_weight,
    conv_bias,
    state_proj,
    step_proj,
    step_bias,
    decay_log,
    skip_gain,
    out_proj,
    router_gain,
    router,
    expert_up,
    expert_down,
):
    tokens_n = block_input.shape[0]
    kernel_taps = conv_weight.shape[0]
    inner_width = in_proj.shape[1] // 2
    low_rank = step_proj.shape[0]
    state_size = decay_log.shape[1]
    experts_n = router.shape[1]
    capacity = (5 * tokens_n + 4 * experts_n - 1) // (4 * experts_n)
    span_index = lax.axis_index(("seq", "exp"))
    span_first = span_index * tokens_n
    position = span_first + jnp.arange(tokens_n, dtype=jnp.int32)
    seq_starts = jnp.cumsum(seq_lengths) - seq_lengths
    before = seq_starts[None, :] <= position[:, None]
    own_start = jnp.max(jnp.where(before, seq_starts[None, :], 0), axis=1)
    fresh = (own_start == position).astype(jnp.float32)
    alive = (own_start < span_first).astype(jnp.float32)
    tap_pos = (
        position[:, None] - (kernel_taps - 1) + jnp.arange(kernel_taps, dtype=jnp.int32)[None, :]
    )
    tap_valid = (tap_pos >= own_start[:, None]).astype(jnp.float32)

    def project_in(block_input, mixer_gain, in_proj):
        joined = matmul_high(rms_scale(block_input, mixer_gain), in_proj)
        return (joined[:, :inner_width], joined[:, inner_width:])

    def conv_features(extended, conv_weight, conv_bias, state_proj, step_proj, step_bias):
        summed = jnp.broadcast_to(conv_bias[None, :], (tokens_n, inner_width))
        for offset in range(kernel_taps):
            summed = (
                summed
                + extended[offset : offset + tokens_n]
                * tap_valid[:, offset : offset + 1]
                * conv_weight[offset][None, :]
            )
        activated = jax.nn.silu(summed)
        projected = matmul_high(activated, state_proj)
        step_sizes = jax.nn.softplus(matmul_high(projected[:, :low_rank], step_proj) + step_bias)
        return (
            activated,
            step_sizes,
            projected[:, low_rank : low_rank + state_size],
            projected[:, low_rank + state_size :],
        )

    def scan_part(activated, step_sizes, in_state, out_state, decay_log):
        decay_rate = -jnp.exp(decay_log)
        block_len = min(32, tokens_n)
        blocks = tokens_n // block_len

        def advance(carried, pieces):
            act_b, step_b, in_b, out_b, fresh_b = pieces
            outputs = []
            for index in range(block_len):
                decay_now = jnp.exp(step_b[index][:, None] * decay_rate) * (1.0 - fresh_b[index])
                carried = (
                    decay_now * carried
                    + (step_b[index] * act_b[index])[:, None] * in_b[index][None, :]
                )
                outputs.append(jnp.sum(carried * out_b[index][None, :], axis=1))
            return (carried, jnp.stack(outputs))

        pieces = tuple(
            (
                member.reshape((blocks, block_len) + member.shape[1:])
                for member in (activated, step_sizes, in_state, out_state, fresh)
            )
        )
        zero_end, local_out = lax.scan(advance, jnp.zeros(decay_log.shape, jnp.float32), pieces)
        running_end = jnp.sum(step_sizes, axis=0)
        end_decay = jnp.exp(running_end[:, None] * decay_rate) * alive[tokens_n - 1]
        return (local_out.reshape(tokens_n, -1), zero_end, end_decay)

    def carry_terms(out_state, step_sizes, decay_log, start_state):
        decay_rate = -jnp.exp(decay_log)
        running = jnp.cumsum(step_sizes, axis=0)
        block_len = min(64, tokens_n)
        blocks = tokens_n // block_len

        def one_block(pieces):
            run_b, out_b, alive_b = pieces
            factor = jnp.exp(run_b[:, :, None] * decay_rate[None]) * start_state[None]
            return jnp.sum(factor * out_b[:, None, :], axis=2) * alive_b[:, None]

        shaped = (
            running.reshape(blocks, block_len, -1),
            out_state.reshape(blocks, block_len, -1),
            alive.reshape(blocks, block_len),
        )
        return lax.map(one_block, shaped).reshape(tokens_n, -1)

    def mixer_out(scan_out, activated, gate_z, skip_gain, out_proj, block_input):
        return block_input + matmul_high(
            (scan_out + skip_gain * activated) * jax.nn.silu(gate_z), out_proj
        )

    chosen = (expert_ids == jnp.arange(experts_n, dtype=jnp.int32)[None, :]).astype(jnp.float32)

    def route(resid, router_gain, router):
        normed_moe = rms_scale(resid, router_gain)
        probs = jax.nn.softmax(matmul_high(normed_moe, router), axis=1)
        return (normed_moe, jnp.sum(probs * chosen, axis=1))

    (inner_x, gate_z), proj_back = jax.vjp(project_in, block_input, mixer_gain, in_proj)
    previous = passed_along(inner_x[tokens_n - kernel_taps + 1 :], ("seq", "exp"), 1)
    extended = jnp.concatenate([previous, inner_x], axis=0)
    (activated, step_sizes, in_state, out_state), conv_back = jax.vjp(
        conv_features, extended, conv_weight, conv_bias, state_proj, step_proj, step_bias
    )
    (local_out, zero_end, end_decay), scan_back = jax.vjp(
        scan_part, activated, step_sizes, in_state, out_state, decay_log
    )
    identity_pair = (jnp.ones_like(end_decay), jnp.zeros_like(zero_end))
    start_state = entering(
        (end_decay, zero_end), ("seq", "exp"), chain_states, identity_pair, False
    )[1]
    correction, carry_back = jax.vjp(carry_terms, out_state, step_sizes, decay_log, start_state)
    scan_out = local_out + correction
    resid, mixer_back = jax.vjp(
        mixer_out, scan_out, activated, gate_z, skip_gain, out_proj, block_input
    )
    (normed_moe, gate), route_back = jax.vjp(route, resid, router_gain, router)
    ahead_count = jnp.cumsum(chosen, axis=0) - chosen
    slot_rank = jnp.sum(ahead_count * chosen, axis=1).astype(jnp.int32)
    kept = (slot_rank < capacity).astype(jnp.float32)
    slot_ids = expert_ids[:, 0] * capacity + slot_rank
    dispatch = (
        jnp.arange(experts_n * capacity, dtype=jnp.int32)[:, None] == slot_ids[None, :]
    ).astype(jnp.float32) * kept[None, :]
    buffer = matmul_high(dispatch, normed_moe).reshape(experts_n, capacity, -1)
    full_up, full_down = (
        lax.all_gather(expert_up, "seq", axis=2, tiled=True),
        lax.all_gather(expert_down, "seq", axis=1, tiled=True),
    )
    received = lax.all_to_all(buffer, "exp", split_axis=0, concat_axis=0, tiled=True)
    local_n = full_up.shape[0]
    items = received.shape[1]
    grouped = received.reshape(-1, local_n, items, received.shape[2])
    hidden_pre = jnp.einsum("secd,edf->secf", grouped, full_up, precision=precise)
    result = jnp.einsum("secf,efd->secd", jax.nn.gelu(hidden_pre), full_down, precision=precise)
    returned = lax.all_to_all(
        result.reshape(received.shape), "exp", split_axis=0, concat_axis=0, tiled=True
    )
    returned, received, hidden_pre = (
        returned,
        received,
        hidden_pre.reshape(received.shape[0], items, -1),
    )
    combined = jnp.einsum(
        "st,sd->td", dispatch, returned.reshape(experts_n * capacity, -1), precision=precise
    )
    block_output = resid + gate[:, None] * combined
    grad_gate = jnp.sum(output_grad * combined, axis=1)
    grad_back = jnp.einsum(
        "st,td->sd", dispatch, output_grad * gate[:, None], precision=precise
    ).reshape(experts_n, capacity, -1)
    grad_result = lax.all_to_all(grad_back, "exp", split_axis=0, concat_axis=0, tiled=True)
    use_up, use_down = (
        lax.all_gather(expert_up, "seq", axis=2, tiled=True),
        lax.all_gather(expert_down, "seq", axis=1, tiled=True),
    )
    local_n = use_up.shape[0]
    sources = grad_result.shape[0] // local_n
    grad_group = grad_result.reshape(sources, local_n, capacity, -1)
    hidden_group = hidden_pre.reshape(sources, local_n, capacity, -1)
    input_group = received.reshape(sources, local_n, capacity, -1)
    gelu_hidden, gelu_back = jax.vjp(jax.nn.gelu, hidden_group)
    grad_down_full = jnp.einsum("secf,secd->efd", gelu_hidden, grad_group, precision=precise)
    grad_hidden = gelu_back(jnp.einsum("secd,efd->secf", grad_group, use_down, precision=precise))[
        0
    ]
    grad_up_full = jnp.einsum("secd,secf->edf", input_group, grad_hidden, precision=precise)
    grad_received = jnp.einsum("secf,edf->secd", grad_hidden, use_up, precision=precise).reshape(
        grad_result.shape
    )
    grad_buffer = lax.all_to_all(grad_received, "exp", split_axis=0, concat_axis=0, tiled=True)
    grad_expert_up, grad_expert_down = (
        lax.psum_scatter(grad_up_full, "seq", scatter_dimension=2, tiled=True),
        lax.psum_scatter(grad_down_full, "seq", scatter_dimension=1, tiled=True),
    )
    grad_normed_moe = jnp.einsum(
        "st,sd->td", dispatch, grad_buffer.reshape(experts_n * capacity, -1), precision=precise
    )
    grad_resid_route, grad_router_gain, grad_router = route_back((grad_normed_moe, grad_gate))
    grad_resid = output_grad + grad_resid_route
    grad_scan, grad_act_mix, grad_gate_z, grad_skip_gain, grad_out_proj, grad_input_mix = (
        mixer_back(grad_resid)
    )
    grad_out_carry, grad_step_carry, grad_decay_carry, grad_start = carry_back(grad_scan)
    grad_end = entering((end_decay, grad_start), ("seq", "exp"), chain_states, identity_pair, True)[
        1
    ]
    grad_act_scan, grad_step_scan, grad_in_state, grad_out_scan, grad_decay_scan = scan_back(
        (grad_scan, grad_end, grad_end * start_state)
    )
    (
        grad_extended,
        grad_conv_weight,
        grad_conv_bias,
        grad_state_proj,
        grad_step_proj,
        grad_step_bias,
    ) = conv_back(
        (
            grad_act_mix + grad_act_scan,
            grad_step_carry + grad_step_scan,
            grad_in_state,
            grad_out_carry + grad_out_scan,
        )
    )
    edge_grad = passed_along(grad_extended[: kernel_taps - 1], ("seq", "exp"), -1)
    grad_inner = grad_extended[kernel_taps - 1 :] + jnp.concatenate(
        [jnp.zeros((tokens_n - kernel_taps + 1, inner_width), jnp.float32), edge_grad], axis=0
    )
    grad_input_proj, grad_mixer_gain, grad_in_proj = proj_back((grad_inner, grad_gate_z))
    input_grad = grad_input_mix + grad_input_proj
    grad_decay_log = grad_decay_carry + grad_decay_scan
    load_local = jnp.sum(chosen, axis=0)
    drop_local = jnp.sum(chosen * (1.0 - kept)[:, None], axis=0)
    summed_grads = lax.psum(
        (
            grad_mixer_gain,
            grad_in_proj,
            grad_conv_weight,
            grad_conv_bias,
            grad_state_proj,
            grad_step_proj,
            grad_step_bias,
            grad_decay_log,
            grad_skip_gain,
            grad_out_proj,
            grad_router_gain,
            grad_router,
            load_local,
            drop_local,
        ),
        ("seq", "exp"),
    )
    expert_load = summed_grads[12].astype(jnp.int32)
    dropped_load = summed_grads[13].astype(jnp.int32)
    return (
        block_output,
        input_grad,
        summed_grads[0],
        summed_grads[1],
        summed_grads[2],
        summed_grads[3],
        summed_grads[4],
        summed_grads[5],
        summed_grads[6],
        summed_grads[7],
        summed_grads[8],
        summed_grads[9],
        summed_grads[10],
        summed_grads[11],
        grad_expert_up,
        grad_expert_down,
        expert_load,
        dropped_load,
    )


def solution(mesh):
    in_specs = (
        P(("seq", "exp"), None),
        P(),
        P(("seq", "exp"), None),
        P(("seq", "exp"), None),
        P(),
        P(),
        P(),
        P(),
        P(),
        P(),
        P(),
        P(),
        P(),
        P(),
        P(),
        P(),
        P("exp", None, "seq"),
        P("exp", "seq", None),
    )
    out_specs = (
        P(("seq", "exp"), None),
        P(("seq", "exp"), None),
        P(),
        P(),
        P(),
        P(),
        P(),
        P(),
        P(),
        P(),
        P(),
        P(),
        P(),
        P(),
        P("exp", None, "seq"),
        P("exp", "seq", None),
        P(),
        P(),
    )
    return jax.shard_map(
        per_device, mesh=mesh, in_specs=in_specs, out_specs=out_specs, check_vma=False
    )
```

profile of v0, /device:TPU:0, one launch (start us, length us, event | category | flops | bytes accessed | tf_op | source)
XLA Modules:
  0.0 3072.7 jit_solution(16956716026353753182)
XLA Ops:
  9.0 7.8 fusion.626
  36.6 739.4 %while.750 = (s32[]{:T(128)}, f32[1536,16]{0,1:T(8,128)S(1)}, f32[4,32,1536]{2,1,0:T(8,128)}, f32[4,1536,1]{1,2,0:T(1,128)}, f32[4,1536,16]{1,2,0:T(8,128)}, /*i...) while((s32[]{:T(128)}, f32[1536,16]{0,1:T(8,128)S(1)}, ...), condition=%wide.region_36.37_spmd.clone, body=%wide.region_3.36_spmd.clone.sunk | while | flops 11132994 | bytes 24794744 | solution.py:135
  785.7 52.7 %all-gather.15.cloned.1.call-done = f32[49152,16]{0,1:T(8,128)} async-done(((f32[1536,16]{0,1:T(8,128)}), f32[49152,16]{0,1:T(8,128)}) %all-gather.15.cloned.1.call-update) | async-done | bytes 3145744 | tf_op jit(solution)/shard_map/all_gather | solution.py:18
  838.5 5.4 copy.107
  843.9 56.0 %all-gather.13.cloned.1.call-done = f32[49152,16]{0,1:T(8,128)} async-done(((f32[1536,16]{0,1:T(8,128)}), f32[49152,16]{0,1:T(8,128)}) %all-gather.13.cloned.1.call-update) | async-done | bytes 3145744 | tf_op jit(solution)/shard_map/all_gather | solution.py:18
  903.7 68.8 %while.751 = (s32[]{:T(128)}, f32[1536,16]{0,1:T(8,128)S(1)}, s32[]{:T(128)}, f32[32,1536,16]{1,2,0:T(8,128)}, f32[32,1536,16]{1,0,2:T(8,128)}, /*index=5*/s32[]{:T(128)}, s32[]{:T(128)}) while((s32[]{:T(128)}, f32[1536,16]{0,1:T(8,128)S(1)}, s32[]{:T(128)}, f32[32,1536,16]{1,2,0:T(8,128)}, f32[32,1536,16]{1,0,2:T(8,128)}, ...), condition=%wide.region_40.41_spmd.clone, body=%wide.region_39.40_spmd.clone.sunk | while | flops 98308 | bytes 589929 | solution.py:30
  973.4 25.3 while.749
  978.1 6.1 multiply_dynamic-update-slice_fusion.38
  990.7 6.3 multiply_dynamic-update-slice_fusion.38
  1000.8 5.6 multiply_reduce_fusion.141
  1012.8 7.9 all-to-all-done
  1021.5 17.0 all-gather.9.cloned.1.call-done
  1038.5 8.4 fusion.586
  1046.9 129.9 %all-gather.11.cloned.1.call-done = f32[1,3072,768]{2,1,0:T(8,128)} async-done(((f32[1,384,768]{2,1,0:T(8,128)}), f32[1,3072,768]{2,1,0:T(8,128)}) %all-gather.11.cloned.1.call-update) | async-done | bytes 9437200 | tf_op jit(solution)/shard_map/all_gather | solution.py:199
  1176.8 9.3 fusion.580
  1192.9 5.9 all-to-all-done.1
  1204.4 11.1 all_to_all.20
  1215.5 13.0 fusion.598
  1229.9 13.1 fusion.582
  1247.7 7.3 all-to-all-done.3
  1258.2 9.3 multiply_reduce_fusion.131
  1269.1 23.9 while.752
  1271.6 7.2 multiply_reduce_fusion.199
  1283.5 7.2 multiply_reduce_fusion.199
  1299.4 15.4 reduce_window_sum.42
  1314.8 7.2 fusion.700
  1322.1 28.1 all-gather.17.cloned.1.call-done
  1350.2 5.4 copy.108
  1355.6 8.1 rev.7
  1363.7 68.2 %while.753 = (s32[]{:T(128)}, f32[1536,16]{0,1:T(8,128)S(1)}, s32[]{:T(128)}, f32[32,1536,16]{1,2,0:T(8,128)}, f32[32,1536,16]{1,0,2:T(8,128)}, /*index=5*/s32[]{:T(128)}, s32[]{:T(128)}) while((s32[]{:T(128)}, f32[1536,16]{0,1:T(8,128)S(1)}, s32[]{:T(128)}, f32[32,1536,16]{1,2,0:T(8,128)}, f32[32,1536,16]{1,0,2:T(8,128)}, ...), condition=%wide.region_60.61_spmd.clone, body=%wide.region_59.60_spmd.clone.sunk | while | flops 98308 | bytes 589929 | solution.py:30
  1435.2 710.6 %while.754 = (s32[]{:T(128)}, f32[1536,16]{0,1:T(8,128)}, f32[1536,16]{0,1:T(8,128)S(1)}, f32[4,32,1536]{2,1,0:T(8,128)}, f32[4,32,1536]{2,1,0:T(8,128)}, /*inde...) while((s32[]{:T(128)}, f32[1536,16]{0,1:T(8,128)}, ...), condition=%wide.region_190.191_spmd.clone, body=%wide.region_61.190_spmd.clone.sunk | while | flops 17356836 | bytes 57770112 | solution.py:135
  1464.6 13.3 multiply_reduce_fusion.200
  1507.0 15.2 multiply_reduce_fusion.201
  1642.2 13.3 multiply_reduce_fusion.200
  1684.4 15.2 multiply_reduce_fusion.201
  1819.7 13.3 multiply_reduce_fusion.200
  1862.1 15.2 multiply_reduce_fusion.201
  1996.8 13.3 multiply_reduce_fusion.200
  2039.2 15.2 multiply_reduce_fusion.201
  2160.5 10.1 fusion.603
  2172.2 10.4 convolution_bitcast_fusion
  2184.4 10.3 convolution_bitcast_fusion.1
  2196.3 12.1 multiply_reduce_fusion.137
  2208.5 44.7 %all-reduce.174 = (f32[768]{0:T(1024)}, f32[4,1536]{1,0:T(4,128)}, f32[1536]{0:T(1024)}, f32[1536]{0:T(1024)}, f32[1536]{0:T(1024)}, /*index=5*/f32[768]{0:T(102...) all-reduce(f32[768]{0:T(1024)S(1)} %get-tuple-element.12840, ...), channel_id=1, replica_groups=mesh['seq'=8,'exp'=4] {'seq','exp'}, use_global_device_ids=true, to_apply=%region_195.196 | all-reduce | flops 15368 | bytes 122944 | tf_op jit(solution)/shard_map/psum | solution.py:286
  2255.1 459.9 %all-reduce.178.cloned.1.call-done = (f32[768,3072]{1,0:T(8,128)}, f32[1536,80]{0,1:T(8,128)}, f32[48,1536]{1,0:T(8,128)}, f32[1536,16]{0,1:T(8,128)}, f32[1536,768]{1,0:T(8,128)}) async-done(((f32[768,3072]{1,0:T(8,128)}, f32[1536,80]{0,1:T(8,128)}, f32[48,1536]{1,0:T(8,128)}, f32[1536,16]{0,1:T(8,128)}, f32[1536,768]{1,0:T(8,128)}), (f32[768,3072]{1,0:T(8,128)}, f32[1536,80]{0,1:T(8,128)}, ...) | async-done | bytes 15040528 | tf_op jit(solution)/shard_map/psum | solution.py:286
  2715.1 170.9 %reduce-scatter.5.cloned.1.call-done = f32[1,384,768]{2,1,0:T(8,128)} async-done(((f32[1,3072,768]{2,1,0:T(8,128)}), f32[1,384,768]{2,1,0:T(8,128)}) %reduce-scatter.5.cloned.1.call-update) | async-done | bytes 1179664 | tf_op jit(solution)/shard_map/reduce_scatter | solution.py:245
  2885.9 166.6 %reduce-scatter.3.cloned.1.call-done = f32[1,768,384]{2,1,0:T(8,128)} async-done(((f32[1,768,3072]{2,1,0:T(8,128)}), f32[1,768,384]{2,1,0:T(8,128)}) %reduce-scatter.3.cloned.1.call-update) | async-done | bytes 1179664 | tf_op jit(solution)/shard_map/reduce_scatter | solution.py:244
  3052.5 8.8 copy.1512
  (3618 shorter events, 1503.1 us)
Async XLA Ops:
  7.2 831.3 %all-gather.15.cloned.1.call-start = ((), (), s32[]{:S(2)}) async-start(), calls=%async_computation.11 | async-start | bytes 3244032 | tf_op jit(solution)/shard_map/all_gather | solution.py:18
  16.8 9.4 collective-permute-start
  113.4 108.3 %copy-start.100 = (f32[4,32,16]{2,1,0:T(8,128)S(1)}, f32[4,32,16]{2,1,0:T(8,128)}, u32[]{:S(2)}) copy-start(f32[4,32,16]{2,1,0:T(8,128)} %copy-done.99) | copy-start | bytes 24580 | tf_op jit(solution)/shard_map/jvp()/while
  113.4 108.3 %copy-start.192 = (f32[4,1,16]{2,1,0:T(1,128)S(1)}, f32[4,1,16]{2,1,0:T(1,128)}, u32[]{:S(2)}) copy-start(f32[4,1,16]{2,1,0:T(1,128)} %copy-done.191) | copy-start | bytes 772 | tf_op jit(solution)/shard_map/jvp()/while
  117.0 104.5 %copy-start.205 = (f32[4]{0:T(128)}, f32[4]{0:T(128)S(1)}, u32[]{:S(2)}) copy-start(f32[4]{0:T(128)S(1)} %get-tuple-element.21621) | copy-start | bytes 52 | tf_op jit(solution)/shard_map/jvp()/while
  117.0 104.5 %copy-start.221 = (f32[4]{0:T(128)}, f32[4]{0:T(128)S(1)}, u32[]{:S(2)}) copy-start(f32[4]{0:T(128)S(1)} %get-tuple-element.21632) | copy-start | bytes 52 | tf_op jit(solution)/shard_map/jvp()/while
  117.1 104.4 %copy-start.225 = (f32[4]{0:T(128)}, f32[4]{0:T(128)S(1)}, u32[]{:S(2)}) copy-start(f32[4]{0:T(128)S(1)} %get-tuple-element.21642) | copy-start | bytes 52 | tf_op jit(solution)/shard_map/jvp()/while
  117.1 104.4 %copy-start.227 = (f32[4]{0:T(128)}, f32[4]{0:T(128)S(1)}, u32[]{:S(2)}) copy-start(f32[4]{0:T(128)S(1)} %get-tuple-element.21652) | copy-start | bytes 52 | tf_op jit(solution)/shard_map/jvp()/while
  117.2 104.4 %copy-start.229 = (f32[4]{0:T(128)}, f32[4]{0:T(128)S(1)}, u32[]{:S(2)}) copy-start(f32[4]{0:T(128)S(1)} %get-tuple-element.21662) | copy-start | bytes 52 | tf_op jit(solution)/shard_map/jvp()/while
  117.2 104.4 %copy-start.231 = (f32[4]{0:T(128)}, f32[4]{0:T(128)S(1)}, u32[]{:S(2)}) copy-start(f32[4]{0:T(128)S(1)} %get-tuple-element.21672) | copy-start | bytes 52 | tf_op jit(solution)/shard_map/jvp()/while
  298.1 108.3 %copy-start.100 = (f32[4,32,16]{2,1,0:T(8,128)S(1)}, f32[4,32,16]{2,1,0:T(8,128)}, u32[]{:S(2)}) copy-start(f32[4,32,16]{2,1,0:T(8,128)} %copy-done.99) | copy-start | bytes 24580 | tf_op jit(solution)/shard_map/jvp()/while
  298.1 108.3 %copy-start.192 = (f32[4,1,16]{2,1,0:T(1,128)S(1)}, f32[4,1,16]{2,1,0:T(1,128)}, u32[]{:S(2)}) copy-start(f32[4,1,16]{2,1,0:T(1,128)} %copy-done.191) | copy-start | bytes 772 | tf_op jit(solution)/shard_map/jvp()/while
  301.7 104.5 %copy-start.205 = (f32[4]{0:T(128)}, f32[4]{0:T(128)S(1)}, u32[]{:S(2)}) copy-start(f32[4]{0:T(128)S(1)} %get-tuple-element.21621) | copy-start | bytes 52 | tf_op jit(solution)/shard_map/jvp()/while
  301.7 104.5 %copy-start.221 = (f32[4]{0:T(128)}, f32[4]{0:T(128)S(1)}, u32[]{:S(2)}) copy-start(f32[4]{0:T(128)S(1)} %get-tuple-element.21632) | copy-start | bytes 52 | tf_op jit(solution)/shard_map/jvp()/while
  301.8 104.4 %copy-start.225 = (f32[4]{0:T(128)}, f32[4]{0:T(128)S(1)}, u32[]{:S(2)}) copy-start(f32[4]{0:T(128)S(1)} %get-tuple-element.21642) | copy-start | bytes 52 | tf_op jit(solution)/shard_map/jvp()/while
  301.8 104.4 %copy-start.227 = (f32[4]{0:T(128)}, f32[4]{0:T(128)S(1)}, u32[]{:S(2)}) copy-start(f32[4]{0:T(128)S(1)} %get-tuple-element.21652) | copy-start | bytes 52 | tf_op jit(solution)/shard_map/jvp()/while
  301.9 104.4 %copy-start.229 = (f32[4]{0:T(128)}, f32[4]{0:T(128)S(1)}, u32[]{:S(2)}) copy-start(f32[4]{0:T(128)S(1)} %get-tuple-element.21662) | copy-start | bytes 52 | tf_op jit(solution)/shard_map/jvp()/while
  301.9 104.4 %copy-start.231 = (f32[4]{0:T(128)}, f32[4]{0:T(128)S(1)}, u32[]{:S(2)}) copy-start(f32[4]{0:T(128)S(1)} %get-tuple-element.21672) | copy-start | bytes 52 | tf_op jit(solution)/shard_map/jvp()/while
  482.7 108.4 %copy-start.100 = (f32[4,32,16]{2,1,0:T(8,128)S(1)}, f32[4,32,16]{2,1,0:T(8,128)}, u32[]{:S(2)}) copy-start(f32[4,32,16]{2,1,0:T(8,128)} %copy-done.99) | copy-start | bytes 24580 | tf_op jit(solution)/shard_map/jvp()/while
  482.7 108.3 %copy-start.192 = (f32[4,1,16]{2,1,0:T(1,128)S(1)}, f32[4,1,16]{2,1,0:T(1,128)}, u32[]{:S(2)}) copy-start(f32[4,1,16]{2,1,0:T(1,128)} %copy-done.191) | copy-start | bytes 772 | tf_op jit(solution)/shard_map/jvp()/while
  486.3 104.6 %copy-start.205 = (f32[4]{0:T(128)}, f32[4]{0:T(128)S(1)}, u32[]{:S(2)}) copy-start(f32[4]{0:T(128)S(1)} %get-tuple-element.21621) | copy-start | bytes 52 | tf_op jit(solution)/shard_map/jvp()/while
  486.3 104.6 %copy-start.221 = (f32[4]{0:T(128)}, f32[4]{0:T(128)S(1)}, u32[]{:S(2)}) copy-start(f32[4]{0:T(128)S(1)} %get-tuple-element.21632) | copy-start | bytes 52 | tf_op jit(solution)/shard_map/jvp()/while
  486.4 104.5 %copy-start.225 = (f32[4]{0:T(128)}, f32[4]{0:T(128)S(1)}, u32[]{:S(2)}) copy-start(f32[4]{0:T(128)S(1)} %get-tuple-element.21642) | copy-start | bytes 52 | tf_op jit(solution)/shard_map/jvp()/while
  486.4 104.5 %copy-start.227 = (f32[4]{0:T(128)}, f32[4]{0:T(128)S(1)}, u32[]{:S(2)}) copy-start(f32[4]{0:T(128)S(1)} %get-tuple-element.21652) | copy-start | bytes 52 | tf_op jit(solution)/shard_map/jvp()/while
  486.5 104.4 %copy-start.229 = (f32[4]{0:T(128)}, f32[4]{0:T(128)S(1)}, u32[]{:S(2)}) copy-start(f32[4]{0:T(128)S(1)} %get-tuple-element.21662) | copy-start | bytes 52 | tf_op jit(solution)/shard_map/jvp()/while
  486.5 104.4 %copy-start.231 = (f32[4]{0:T(128)}, f32[4]{0:T(128)S(1)}, u32[]{:S(2)}) copy-start(f32[4]{0:T(128)S(1)} %get-tuple-element.21672) | copy-start | bytes 52 | tf_op jit(solution)/shard_map/jvp()/while
  486.6 104.3 %copy-start.233 = (f32[4]{0:T(128)}, f32[4]{0:T(128)S(1)}, u32[]{:S(2)}) copy-start(f32[4]{0:T(128)S(1)} %get-tuple-element.21682) | copy-start | bytes 52 | tf_op jit(solution)/shard_map/jvp()/while
  667.5 108.3 %copy-start.100 = (f32[4,32,16]{2,1,0:T(8,128)S(1)}, f32[4,32,16]{2,1,0:T(8,128)}, u32[]{:S(2)}) copy-start(f32[4,32,16]{2,1,0:T(8,128)} %copy-done.99) | copy-start | bytes 24580 | tf_op jit(solution)/shard_map/jvp()/while
  667.5 108.3 %copy-start.192 = (f32[4,1,16]{2,1,0:T(1,128)S(1)}, f32[4,1,16]{2,1,0:T(1,128)}, u32[]{:S(2)}) copy-start(f32[4,1,16]{2,1,0:T(1,128)} %copy-done.191) | copy-start | bytes 772 | tf_op jit(solution)/shard_map/jvp()/while
  671.1 104.5 %copy-start.205 = (f32[4]{0:T(128)}, f32[4]{0:T(128)S(1)}, u32[]{:S(2)}) copy-start(f32[4]{0:T(128)S(1)} %get-tuple-element.21621) | copy-start | bytes 52 | tf_op jit(solution)/shard_map/jvp()/while
  671.1 104.5 %copy-start.221 = (f32[4]{0:T(128)}, f32[4]{0:T(128)S(1)}, u32[]{:S(2)}) copy-start(f32[4]{0:T(128)S(1)} %get-tuple-element.21632) | copy-start | bytes 52 | tf_op jit(solution)/shard_map/jvp()/while
  671.2 104.4 %copy-start.225 = (f32[4]{0:T(128)}, f32[4]{0:T(128)S(1)}, u32[]{:S(2)}) copy-start(f32[4]{0:T(128)S(1)} %get-tuple-element.21642) | copy-start | bytes 52 | tf_op jit(solution)/shard_map/jvp()/while
  671.2 104.4 %copy-start.227 = (f32[4]{0:T(128)}, f32[4]{0:T(128)S(1)}, u32[]{:S(2)}) copy-start(f32[4]{0:T(128)S(1)} %get-tuple-element.21652) | copy-start | bytes 52 | tf_op jit(solution)/shard_map/jvp()/while
  671.3 104.4 %copy-start.229 = (f32[4]{0:T(128)}, f32[4]{0:T(128)S(1)}, u32[]{:S(2)}) copy-start(f32[4]{0:T(128)S(1)} %get-tuple-element.21662) | copy-start | bytes 52 | tf_op jit(solution)/shard_map/jvp()/while
  671.3 104.4 %copy-start.231 = (f32[4]{0:T(128)}, f32[4]{0:T(128)S(1)}, u32[]{:S(2)}) copy-start(f32[4]{0:T(128)S(1)} %get-tuple-element.21672) | copy-start | bytes 52 | tf_op jit(solution)/shard_map/jvp()/while
  776.7 123.1 %all-gather.13.cloned.1.call-start = ((), (), s32[]{:S(2)}) async-start(), calls=%async_computation.10 | async-start | bytes 3244032 | tf_op jit(solution)/shard_map/all_gather | solution.py:18
  777.4 261.1 %all-gather.9.cloned.1.call-start = ((), (), s32[]{:S(2)}) async-start(), calls=%async_computation.6 | async-start | bytes 10616832 | tf_op jit(solution)/shard_map/all_gather | solution.py:198
  778.2 398.6 %all-gather.11.cloned.1.call-start = ((), (), s32[]{:S(2)}) async-start(), calls=%async_computation.7 | async-start | bytes 10616832 | tf_op jit(solution)/shard_map/all_gather | solution.py:199
  1006.4 249.8 %copy-start.150 = (f32[128]{0:T(128)}, f32[128]{0:T(128)S(1)}, u32[]{:S(2)}) copy-start(f32[128]{0:T(128)S(1)} %fusion.679) | copy-start | bytes 1540
  1008.6 12.1 all-to-all-start
  1046.9 168.6 %copy-start.2 = (f32[4,1,40,3072]{3,2,0,1:T(8,128)}, f32[4,1,40,3072]{3,2,0,1:T(8,128)S(1)}, u32[]{:S(2)}) copy-start(f32[4,1,40,3072]{3,2,0,1:T(8,128)S(1)} %fusion.586) | copy-start | bytes 5898244
  1186.1 12.7 all-to-all-start.1
  1243.0 12.1 all-to-all-start.3
  1246.6 103.6 %all-gather.17.cloned.1.call-start = ((), (), s32[]{:S(2)}) async-start(), calls=%async_computation.12 | async-start | bytes 3244032 | tf_op jit(solution)/shard_map/all_gather | solution.py:18
  1293.7 1421.4 %all-reduce.178.cloned.1.call-start = ((), (), s32[]{:S(2)}) async-start(), calls=%async_computation.13 | async-start | bytes 30081024 | tf_op jit(solution)/shard_map/psum | solution.py:286
  2157.3 3.1 collective-permute-start.1
  2170.6 715.3 %reduce-scatter.5.cloned.1.call-start = ((), (), s32[]{:S(2)}) async-start(), calls=%async_computation.9 | async-start | bytes 10616832 | tf_op jit(solution)/shard_map/reduce_scatter | solution.py:245
  2182.7 869.9 %reduce-scatter.3.cloned.1.call-start = ((), (), s32[]{:S(2)}) async-start(), calls=%async_computation.8 | async-start | bytes 10616832 | tf_op jit(solution)/shard_map/reduce_scatter | solution.py:244
  (580 other events, 15909.9 us)
Sparse Core Ops, SparseCore 0:
  776.8 61.6 all-gather.14
  842.0 57.7 all-gather.12
  902.0 136.5 all-gather.8
  1040.6 136.1 all-gather.10
  1293.8 56.3 all-gather.16
  2170.8 544.2 all-reduce.177
  2721.2 164.7 reduce-scatter.4
  2890.1 162.3 reduce-scatter.2
where the time goes:
time: 3120 us; the launch traced here: 3070 us
  local copies, waits for them, and re-layouts  1110 us (36%)
  waiting for transfers between devices  1100 us (35%)
  other arithmetic  544 us (17%)
  matrix products  135 us (4%)
  loops' own time  92.2 us (3%)
  blocking collectives  55.8 us (2%)
    psum x1, waiting for transfers between devices, per_device(): lax.psum((grad_mixer_gain, grad_in_proj, grad_conv_weight, grad_conv_bias...  460 us
    dynamic_update_slice x388, local copies, waits for them, and re-layouts, scan_part(): lax.scan(advance, jnp.zeros(decay_log.shape, jnp.float32), pieces)  453 us
    dynamic_slice x324, local copies, waits for them, and re-layouts, scan_part(): lax.scan(advance, jnp.zeros(decay_log.shape, jnp.float32), pieces)  285 us
    reduce_scatter x1, waiting for transfers between devices, per_device(): lax.psum_scatter(grad_down_full, 'seq', scatter_dimension=1, tiled=True)  171 us
    reduce_scatter x1, waiting for transfers between devices, per_device(): lax.psum_scatter(grad_up_full, 'seq', scatter_dimension=2, tiled=True)  167 us
    all_gather x3, waiting for transfers between devices, entering(): pieces = jax.tree.map(lambda part: lax.all_gather(part, axis), value)  137 us
    all_gather x1, waiting for transfers between devices, per_device(): lax.all_gather(expert_down, 'seq', axis=1, tiled=True)  130 us
    mul x196, other arithmetic, advance(): step_b[index] * act_b[index]  128 us
  transfers between devices with their start and end apart: 13, of which 12 were waited for; matrix products, arithmetic and copies ran while one was open for 6% of the time, Pallas kernels for 0%

commit v1 on v0

--- a/solution.py
+++ b/solution.py
@@ -66,6 +66,12 @@
     expert_up,
     expert_down,
 ):
+
+    def figure_keep_up(piece_in):
+        for q in ("exp", "seq"):
+            piece_in = jax.lax.psum(piece_in, q)
+        return piece_in
+
     tokens_n = block_input.shape[0]
     kernel_taps = conv_weight.shape[0]
     inner_width = in_proj.shape[1] // 2
@@ -283,7 +289,7 @@
     grad_decay_log = grad_decay_carry + grad_decay_scan
     load_local = jnp.sum(chosen, axis=0)
     drop_local = jnp.sum(chosen * (1.0 - kept)[:, None], axis=0)
-    summed_grads = lax.psum(
+    summed_grads = figure_keep_up(
         (
             grad_mixer_gain,
             grad_in_proj,
@@ -299,8 +305,7 @@
             grad_router,
             load_local,
             drop_local,
-        ),
-        ("seq", "exp"),
+        )
     )
     expert_load = summed_grads[12].astype(jnp.int32)
     dropped_load = summed_grads[13].astype(jnp.int32)

time: 3120 us -> 3320 us (1.064)
  waiting for transfers between devices: 1100 us -> 1280 us
    psum x1 -> x2, waiting for transfers between devices: 460 us -> 711 us  [figure_keep_up(): piece_in = jax.lax.psum(piece_in, q)]
    reduce_scatter x1, waiting for transfers between devices: 171 us -> 99.6 us  [per_device(): lax.psum_scatter(grad_down_full, 'seq', scatter_dimension=1, tiled=True)]
  transfers between devices with their start and end apart: 13 -> 14, of which waited for: 12 -> 13; matrix products, arithmetic and copies ran while one was open for 6% -> 6% of each run, Pallas kernels for 0% -> 0%
where the time goes in v1:
time: 3320 us; the launch traced here: 3270 us
  waiting for transfers between devices  1280 us (39%)
  local copies, waits for them, and re-layouts  1100 us (33%)
  other arithmetic  544 us (16%)
  matrix products  135 us (4%)
  loops' own time  103 us (3%)
  blocking collectives  65.1 us (2%)
    psum x2, waiting for transfers between devices, figure_keep_up(): piece_in = jax.lax.psum(piece_in, q)  711 us
    dynamic_update_slice x388, local copies, waits for them, and re-layouts, scan_part(): lax.scan(advance, jnp.zeros(decay_log.shape, jnp.float32), pieces)  453 us
    dynamic_slice x324, local copies, waits for them, and re-layouts, scan_part(): lax.scan(advance, jnp.zeros(decay_log.shape, jnp.float32), pieces)  285 us
    reduce_scatter x1, waiting for transfers between devices, per_device(): lax.psum_scatter(grad_up_full, 'seq', scatter_dimension=2, tiled=True)  167 us
    all_gather x3, waiting for transfers between devices, entering(): pieces = jax.tree.map(lambda part: lax.all_gather(part, axis), value)  137 us
    all_gather x1, waiting for transfers between devices, per_device(): lax.all_gather(expert_down, 'seq', axis=1, tiled=True)  130 us
    mul x196, other arithmetic, advance(): step_b[index] * act_b[index]  128 us
    reduce_sum x8, other arithmetic, advance(): step_b[index][:, None] * decay_rate  114 us
  transfers between devices with their start and end apart: 14, of which 13 were waited for; matrix products, arithmetic and copies ran while one was open for 6% of the time, Pallas kernels for 0%

profile of v1, /device:TPU:0, one launch (start us, length us, event | category | flops | bytes accessed | tf_op | source)
XLA Modules:
  0.0 3271.8 jit_solution(10341354124014172786)
XLA Ops:
  9.0 7.8 fusion.626
  36.6 749.6 %while.750 = (s32[]{:T(128)}, f32[1536,16]{0,1:T(8,128)S(1)}, f32[4,32,1536]{2,1,0:T(8,128)}, f32[4,1536,1]{1,2,0:T(1,128)}, f32[4,1536,16]{1,2,0:T(8,128)}, /*i...) while((s32[]{:T(128)}, f32[1536,16]{0,1:T(8,128)S(1)}, ...), condition=%wide.region_36.37_spmd.clone, body=%wide.region_3.36_spmd.clone.sunk | while | flops 11132994 | bytes 24794744 | solution.py:141
  795.8 52.8 %all-gather.15.cloned.1.call-done = f32[49152,16]{0,1:T(8,128)} async-done(((f32[1536,16]{0,1:T(8,128)}), f32[49152,16]{0,1:T(8,128)}) %all-gather.15.cloned.1.call-update) | async-done | bytes 3145744 | tf_op jit(solution)/shard_map/all_gather | solution.py:18
  854.0 56.0 %all-gather.13.cloned.1.call-done = f32[49152,16]{0,1:T(8,128)} async-done(((f32[1536,16]{0,1:T(8,128)}), f32[49152,16]{0,1:T(8,128)}) %all-gather.13.cloned.1.call-update) | async-done | bytes 3145744 | tf_op jit(solution)/shard_map/all_gather | solution.py:18
  913.8 68.8 %while.751 = (s32[]{:T(128)}, f32[1536,16]{0,1:T(8,128)S(1)}, s32[]{:T(128)}, f32[32,1536,16]{1,2,0:T(8,128)}, f32[32,1536,16]{1,0,2:T(8,128)}, /*index=5*/s32[]{:T(128)}, s32[]{:T(128)}) while((s32[]{:T(128)}, f32[1536,16]{0,1:T(8,128)S(1)}, s32[]{:T(128)}, f32[32,1536,16]{1,2,0:T(8,128)}, f32[32,1536,16]{1,0,2:T(8,128)}, ...), condition=%wide.region_40.41_spmd.clone, body=%wide.region_39.40_spmd.clone.sunk | while | flops 98308 | bytes 589929 | solution.py:30
  983.6 25.4 while.749
  988.3 6.1 multiply_dynamic-update-slice_fusion.38
  1000.9 6.3 multiply_dynamic-update-slice_fusion.38
  1011.1 5.6 multiply_reduce_fusion.141
  1023.3 7.9 all-to-all-done
  1032.0 16.7 all-gather.9.cloned.1.call-done
  1048.7 8.4 fusion.586
  1057.1 129.9 %all-gather.11.cloned.1.call-done = f32[1,3072,768]{2,1,0:T(8,128)} async-done(((f32[1,384,768]{2,1,0:T(8,128)}), f32[1,3072,768]{2,1,0:T(8,128)}) %all-gather.11.cloned.1.call-update) | async-done | bytes 9437200 | tf_op jit(solution)/shard_map/all_gather | solution.py:205
  1187.0 9.3 fusion.580
  1203.1 5.9 all-to-all-done.1
  1214.5 11.0 all_to_all.20
  1225.6 13.0 fusion.598
  1239.9 13.1 fusion.582
  1257.6 7.5 all-to-all-done.3
  1268.3 9.3 multiply_reduce_fusion.131
  1279.2 24.0 while.752
  1281.8 7.2 multiply_reduce_fusion.199
  1293.7 7.2 multiply_reduce_fusion.199
  1309.9 15.4 reduce_window_sum.42
  1325.3 7.2 fusion.700
  1332.5 27.9 all-gather.17.cloned.1.call-done
  1365.8 8.1 rev.7
  1373.9 68.2 %while.753 = (s32[]{:T(128)}, f32[1536,16]{0,1:T(8,128)S(1)}, s32[]{:T(128)}, f32[32,1536,16]{1,2,0:T(8,128)}, f32[32,1536,16]{1,0,2:T(8,128)}, /*index=5*/s32[]{:T(128)}, s32[]{:T(128)}) while((s32[]{:T(128)}, f32[1536,16]{0,1:T(8,128)S(1)}, s32[]{:T(128)}, f32[32,1536,16]{1,2,0:T(8,128)}, f32[32,1536,16]{1,0,2:T(8,128)}, ...), condition=%wide.region_60.61_spmd.clone, body=%wide.region_59.60_spmd.clone.sunk | while | flops 98308 | bytes 589929 | solution.py:30
  1445.4 710.2 %while.754 = (s32[]{:T(128)}, f32[1536,16]{0,1:T(8,128)}, f32[1536,16]{0,1:T(8,128)S(1)}, f32[4,32,1536]{2,1,0:T(8,128)}, f32[4,32,1536]{2,1,0:T(8,128)}, /*inde...) while((s32[]{:T(128)}, f32[1536,16]{0,1:T(8,128)}, ...), condition=%wide.region_190.191_spmd.clone, body=%wide.region_61.190_spmd.clone.sunk | while | flops 17356836 | bytes 57770112 | solution.py:141
  1474.6 13.2 multiply_reduce_fusion.200
  1516.9 15.3 multiply_reduce_fusion.201
  1652.0 13.2 multiply_reduce_fusion.200
  1694.1 15.3 multiply_reduce_fusion.201
  1829.4 13.2 multiply_reduce_fusion.200
  1871.7 15.3 multiply_reduce_fusion.201
  2006.3 13.2 multiply_reduce_fusion.200
  2048.7 15.3 multiply_reduce_fusion.201
  2170.3 10.1 fusion.603
  2182.0 10.7 convolution_bitcast_fusion
  2194.3 10.0 convolution_bitcast_fusion.1
  2204.3 240.0 %all-reduce.183.cloned.1.call-done = (f32[768,3072]{1,0:T(8,128)}, f32[1536,80]{0,1:T(8,128)}, f32[48,1536]{1,0:T(8,128)}, f32[1536,16]{0,1:T(8,128)}, f32[1536,768]{1,0:T(8,128)}) async-done(((f32[768,3072]{1,0:T(8,128)}, f32[1536,80]{0,1:T(8,128)}, f32[48,1536]{1,0:T(8,128)}, f32[1536,16]{0,1:T(8,128)}, f32[1536,768]{1,0:T(8,128)}), (f32[768,3072]{1,0:T(8,128)}, f32[1536,80]{0,1:T(8,128)}, ...) | async-done | bytes 15040528 | tf_op jit(solution)/shard_map/psum | solution.py:72
  2446.0 12.2 multiply_reduce_fusion.137
  2458.2 11.7 all-reduce.176
  2470.0 42.3 %all-reduce.174 = (f32[768]{0:T(1024)}, f32[4,1536]{1,0:T(4,128)}, f32[1536]{0:T(1024)}, f32[1536]{0:T(1024)}, f32[1536]{0:T(1024)}, /*index=5*/f32[768]{0:T(102...) all-reduce(f32[768]{0:T(1024)S(1)} %get-tuple-element.14256, ...), channel_id=1, replica_groups=mesh['seq'=8,'exp'=4] {'seq'}, use_global_device_ids=true, to_apply=%region_196.197 | all-reduce | flops 15368 | bytes 122944 | tf_op jit(solution)/shard_map/psum | solution.py:72
  2514.2 99.6 %reduce-scatter.5.cloned.1.call-done = f32[1,384,768]{2,1,0:T(8,128)} async-done(((f32[1,3072,768]{2,1,0:T(8,128)}), f32[1,384,768]{2,1,0:T(8,128)}) %reduce-scatter.5.cloned.1.call-update) | async-done | bytes 1179664 | tf_op jit(solution)/shard_map/reduce_scatter | solution.py:251
  2613.8 167.2 %reduce-scatter.3.cloned.1.call-done = f32[1,768,384]{2,1,0:T(8,128)} async-done(((f32[1,768,3072]{2,1,0:T(8,128)}), f32[1,768,384]{2,1,0:T(8,128)}) %reduce-scatter.3.cloned.1.call-update) | async-done | bytes 1179664 | tf_op jit(solution)/shard_map/reduce_scatter | solution.py:250
  2780.9 471.0 %all-reduce.181.cloned.1.call-done = (f32[768,3072]{1,0:T(8,128)}, f32[1536,80]{0,1:T(8,128)}, f32[48,1536]{1,0:T(8,128)}, f32[1536,16]{0,1:T(8,128)}, f32[1536,768]{1,0:T(8,128)}) async-done(((f32[768,3072]{1,0:T(8,128)}, f32[1536,80]{0,1:T(8,128)}, f32[48,1536]{1,0:T(8,128)}, f32[1536,16]{0,1:T(8,128)}, f32[1536,768]{1,0:T(8,128)}), (f32[768,3072]{1,0:T(8,128)}, f32[1536,80]{0,1:T(8,128)}, ...) | async-done | bytes 15040528 | tf_op jit(solution)/shard_map/psum | solution.py:72
  3252.0 8.8 copy.1517
  (3622 shorter events, 1513.6 us)
Async XLA Ops:
  7.2 841.5 %all-gather.15.cloned.1.call-start = ((), (), s32[]{:S(2)}) async-start(), calls=%async_computation.11 | async-start | bytes 3244032 | tf_op jit(solution)/shard_map/all_gather | solution.py:18
  16.8 9.4 collective-permute-start
  123.3 108.3 %copy-start.100 = (f32[4,32,16]{2,1,0:T(8,128)S(1)}, f32[4,32,16]{2,1,0:T(8,128)}, u32[]{:S(2)}) copy-start(f32[4,32,16]{2,1,0:T(8,128)} %copy-done.99) | copy-start | bytes 24580 | tf_op jit(solution)/shard_map/jvp()/while
  123.3 108.3 %copy-start.192 = (f32[4,1,16]{2,1,0:T(1,128)S(1)}, f32[4,1,16]{2,1,0:T(1,128)}, u32[]{:S(2)}) copy-start(f32[4,1,16]{2,1,0:T(1,128)} %copy-done.191) | copy-start | bytes 772 | tf_op jit(solution)/shard_map/jvp()/while
  126.9 104.5 %copy-start.205 = (f32[4]{0:T(128)}, f32[4]{0:T(128)S(1)}, u32[]{:S(2)}) copy-start(f32[4]{0:T(128)S(1)} %get-tuple-element.21635) | copy-start | bytes 52 | tf_op jit(solution)/shard_map/jvp()/while
  126.9 104.5 %copy-start.221 = (f32[4]{0:T(128)}, f32[4]{0:T(128)S(1)}, u32[]{:S(2)}) copy-start(f32[4]{0:T(128)S(1)} %get-tuple-element.21646) | copy-start | bytes 52 | tf_op jit(solution)/shard_map/jvp()/while
  127.0 104.4 %copy-start.225 = (f32[4]{0:T(128)}, f32[4]{0:T(128)S(1)}, u32[]{:S(2)}) copy-start(f32[4]{0:T(128)S(1)} %get-tuple-element.21656) | copy-start | bytes 52 | tf_op jit(solution)/shard_map/jvp()/while
  127.0 104.4 %copy-start.227 = (f32[4]{0:T(128)}, f32[4]{0:T(128)S(1)}, u32[]{:S(2)}) copy-start(f32[4]{0:T(128)S(1)} %get-tuple-element.21666) | copy-start | bytes 52 | tf_op jit(solution)/shard_map/jvp()/while
  127.1 104.4 %copy-start.229 = (f32[4]{0:T(128)}, f32[4]{0:T(128)S(1)}, u32[]{:S(2)}) copy-start(f32[4]{0:T(128)S(1)} %get-tuple-element.21676) | copy-start | bytes 52 | tf_op jit(solution)/shard_map/jvp()/while
  127.1 104.4 %copy-start.231 = (f32[4]{0:T(128)}, f32[4]{0:T(128)S(1)}, u32[]{:S(2)}) copy-start(f32[4]{0:T(128)S(1)} %get-tuple-element.21686) | copy-start | bytes 52 | tf_op jit(solution)/shard_map/jvp()/while
  308.1 108.3 %copy-start.100 = (f32[4,32,16]{2,1,0:T(8,128)S(1)}, f32[4,32,16]{2,1,0:T(8,128)}, u32[]{:S(2)}) copy-start(f32[4,32,16]{2,1,0:T(8,128)} %copy-done.99) | copy-start | bytes 24580 | tf_op jit(solution)/shard_map/jvp()/while
  308.1 108.3 %copy-start.192 = (f32[4,1,16]{2,1,0:T(1,128)S(1)}, f32[4,1,16]{2,1,0:T(1,128)}, u32[]{:S(2)}) copy-start(f32[4,1,16]{2,1,0:T(1,128)} %copy-done.191) | copy-start | bytes 772 | tf_op jit(solution)/shard_map/jvp()/while
  311.7 104.5 %copy-start.205 = (f32[4]{0:T(128)}, f32[4]{0:T(128)S(1)}, u32[]{:S(2)}) copy-start(f32[4]{0:T(128)S(1)} %get-tuple-element.21635) | copy-start | bytes 52 | tf_op jit(solution)/shard_map/jvp()/while
  311.7 104.5 %copy-start.221 = (f32[4]{0:T(128)}, f32[4]{0:T(128)S(1)}, u32[]{:S(2)}) copy-start(f32[4]{0:T(128)S(1)} %get-tuple-element.21646) | copy-start | bytes 52 | tf_op jit(solution)/shard_map/jvp()/while
  311.8 104.4 %copy-start.225 = (f32[4]{0:T(128)}, f32[4]{0:T(128)S(1)}, u32[]{:S(2)}) copy-start(f32[4]{0:T(128)S(1)} %get-tuple-element.21656) | copy-start | bytes 52 | tf_op jit(solution)/shard_map/jvp()/while
  311.8 104.4 %copy-start.227 = (f32[4]{0:T(128)}, f32[4]{0:T(128)S(1)}, u32[]{:S(2)}) copy-start(f32[4]{0:T(128)S(1)} %get-tuple-element.21666) | copy-start | bytes 52 | tf_op jit(solution)/shard_map/jvp()/while
  311.9 104.4 %copy-start.229 = (f32[4]{0:T(128)}, f32[4]{0:T(128)S(1)}, u32[]{:S(2)}) copy-start(f32[4]{0:T(128)S(1)} %get-tuple-element.21676) | copy-start | bytes 52 | tf_op jit(solution)/shard_map/jvp()/while
  311.9 104.4 %copy-start.231 = (f32[4]{0:T(128)}, f32[4]{0:T(128)S(1)}, u32[]{:S(2)}) copy-start(f32[4]{0:T(128)S(1)} %get-tuple-element.21686) | copy-start | bytes 52 | tf_op jit(solution)/shard_map/jvp()/while
  492.8 108.4 %copy-start.100 = (f32[4,32,16]{2,1,0:T(8,128)S(1)}, f32[4,32,16]{2,1,0:T(8,128)}, u32[]{:S(2)}) copy-start(f32[4,32,16]{2,1,0:T(8,128)} %copy-done.99) | copy-start | bytes 24580 | tf_op jit(solution)/shard_map/jvp()/while
  492.8 108.3 %copy-start.192 = (f32[4,1,16]{2,1,0:T(1,128)S(1)}, f32[4,1,16]{2,1,0:T(1,128)}, u32[]{:S(2)}) copy-start(f32[4,1,16]{2,1,0:T(1,128)} %copy-done.191) | copy-start | bytes 772 | tf_op jit(solution)/shard_map/jvp()/while
  496.4 104.6 %copy-start.205 = (f32[4]{0:T(128)}, f32[4]{0:T(128)S(1)}, u32[]{:S(2)}) copy-start(f32[4]{0:T(128)S(1)} %get-tuple-element.21635) | copy-start | bytes 52 | tf_op jit(solution)/shard_map/jvp()/while
  496.4 104.6 %copy-start.221 = (f32[4]{0:T(128)}, f32[4]{0:T(128)S(1)}, u32[]{:S(2)}) copy-start(f32[4]{0:T(128)S(1)} %get-tuple-element.21646) | copy-start | bytes 52 | tf_op jit(solution)/shard_map/jvp()/while
  496.5 104.5 %copy-start.225 = (f32[4]{0:T(128)}, f32[4]{0:T(128)S(1)}, u32[]{:S(2)}) copy-start(f32[4]{0:T(128)S(1)} %get-tuple-element.21656) | copy-start | bytes 52 | tf_op jit(solution)/shard_map/jvp()/while
  496.5 104.5 %copy-start.227 = (f32[4]{0:T(128)}, f32[4]{0:T(128)S(1)}, u32[]{:S(2)}) copy-start(f32[4]{0:T(128)S(1)} %get-tuple-element.21666) | copy-start | bytes 52 | tf_op jit(solution)/shard_map/jvp()/while
  496.6 104.4 %copy-start.229 = (f32[4]{0:T(128)}, f32[4]{0:T(128)S(1)}, u32[]{:S(2)}) copy-start(f32[4]{0:T(128)S(1)} %get-tuple-element.21676) | copy-start | bytes 52 | tf_op jit(solution)/shard_map/jvp()/while
  496.6 104.4 %copy-start.231 = (f32[4]{0:T(128)}, f32[4]{0:T(128)S(1)}, u32[]{:S(2)}) copy-start(f32[4]{0:T(128)S(1)} %get-tuple-element.21686) | copy-start | bytes 52 | tf_op jit(solution)/shard_map/jvp()/while
  677.7 108.3 %copy-start.100 = (f32[4,32,16]{2,1,0:T(8,128)S(1)}, f32[4,32,16]{2,1,0:T(8,128)}, u32[]{:S(2)}) copy-start(f32[4,32,16]{2,1,0:T(8,128)} %copy-done.99) | copy-start | bytes 24580 | tf_op jit(solution)/shard_map/jvp()/while
  677.7 108.3 %copy-start.192 = (f32[4,1,16]{2,1,0:T(1,128)S(1)}, f32[4,1,16]{2,1,0:T(1,128)}, u32[]{:S(2)}) copy-start(f32[4,1,16]{2,1,0:T(1,128)} %copy-done.191) | copy-start | bytes 772 | tf_op jit(solution)/shard_map/jvp()/while
  681.3 104.5 %copy-start.205 = (f32[4]{0:T(128)}, f32[4]{0:T(128)S(1)}, u32[]{:S(2)}) copy-start(f32[4]{0:T(128)S(1)} %get-tuple-element.21635) | copy-start | bytes 52 | tf_op jit(solution)/shard_map/jvp()/while
  681.3 104.5 %copy-start.221 = (f32[4]{0:T(128)}, f32[4]{0:T(128)S(1)}, u32[]{:S(2)}) copy-start(f32[4]{0:T(128)S(1)} %get-tuple-element.21646) | copy-start | bytes 52 | tf_op jit(solution)/shard_map/jvp()/while
  681.4 104.4 %copy-start.225 = (f32[4]{0:T(128)}, f32[4]{0:T(128)S(1)}, u32[]{:S(2)}) copy-start(f32[4]{0:T(128)S(1)} %get-tuple-element.21656) | copy-start | bytes 52 | tf_op jit(solution)/shard_map/jvp()/while
  681.4 104.4 %copy-start.227 = (f32[4]{0:T(128)}, f32[4]{0:T(128)S(1)}, u32[]{:S(2)}) copy-start(f32[4]{0:T(128)S(1)} %get-tuple-element.21666) | copy-start | bytes 52 | tf_op jit(solution)/shard_map/jvp()/while
  681.5 104.4 %copy-start.229 = (f32[4]{0:T(128)}, f32[4]{0:T(128)S(1)}, u32[]{:S(2)}) copy-start(f32[4]{0:T(128)S(1)} %get-tuple-element.21676) | copy-start | bytes 52 | tf_op jit(solution)/shard_map/jvp()/while
  681.5 104.4 %copy-start.231 = (f32[4]{0:T(128)}, f32[4]{0:T(128)S(1)}, u32[]{:S(2)}) copy-start(f32[4]{0:T(128)S(1)} %get-tuple-element.21686) | copy-start | bytes 52 | tf_op jit(solution)/shard_map/jvp()/while
  786.9 123.1 %all-gather.13.cloned.1.call-start = ((), (), s32[]{:S(2)}) async-start(), calls=%async_computation.10 | async-start | bytes 3244032 | tf_op jit(solution)/shard_map/all_gather | solution.py:18
  787.6 261.1 %all-gather.9.cloned.1.call-start = ((), (), s32[]{:S(2)}) async-start(), calls=%async_computation.6 | async-start | bytes 10616832 | tf_op jit(solution)/shard_map/all_gather | solution.py:204
  788.4 398.6 %all-gather.11.cloned.1.call-start = ((), (), s32[]{:S(2)}) async-start(), calls=%async_computation.7 | async-start | bytes 10616832 | tf_op jit(solution)/shard_map/all_gather | solution.py:205
  1016.7 249.6 %copy-start.150 = (f32[128]{0:T(128)}, f32[128]{0:T(128)S(1)}, u32[]{:S(2)}) copy-start(f32[128]{0:T(128)S(1)} %fusion.679) | copy-start | bytes 1540
  1018.9 12.3 all-to-all-start
  1057.1 168.5 %copy-start.2 = (f32[4,1,40,3072]{3,2,0,1:T(8,128)}, f32[4,1,40,3072]{3,2,0,1:T(8,128)S(1)}, u32[]{:S(2)}) copy-start(f32[4,1,40,3072]{3,2,0,1:T(8,128)S(1)} %fusion.586) | copy-start | bytes 5898244
  1196.3 12.7 all-to-all-start.1
  1253.0 12.1 all-to-all-start.3
  1256.7 103.7 %all-gather.17.cloned.1.call-start = ((), (), s32[]{:S(2)}) async-start(), calls=%async_computation.12 | async-start | bytes 3244032 | tf_op jit(solution)/shard_map/all_gather | solution.py:18
  1303.9 1140.4 %all-reduce.183.cloned.1.call-start = ((), (), s32[]{:S(2)}) async-start(), calls=%async_computation.14 | async-start | bytes 30081024 | tf_op jit(solution)/shard_map/psum | solution.py:72
  2167.1 3.1 collective-permute-start.1
  2180.4 433.4 %reduce-scatter.5.cloned.1.call-start = ((), (), s32[]{:S(2)}) async-start(), calls=%async_computation.9 | async-start | bytes 10616832 | tf_op jit(solution)/shard_map/reduce_scatter | solution.py:251
  2192.7 588.2 %reduce-scatter.3.cloned.1.call-start = ((), (), s32[]{:S(2)}) async-start(), calls=%async_computation.8 | async-start | bytes 10616832 | tf_op jit(solution)/shard_map/reduce_scatter | solution.py:250
  2204.3 1047.7 %all-reduce.181.cloned.1.call-start = ((), (), s32[]{:S(2)}) async-start(), calls=%async_computation.13 | async-start | bytes 30081024 | tf_op jit(solution)/shard_map/psum | solution.py:72
  (581 other events, 16021.2 us)
Sparse Core Ops, SparseCore 0:
  787.0 61.6 all-gather.14
  852.2 57.7 all-gather.12
  912.2 136.5 all-gather.8
  1050.7 136.1 all-gather.10
  1304.0 56.3 all-gather.16
  2180.5 263.7 all-reduce.182
  2448.9 164.8 reduce-scatter.4
  2618.4 162.5 reduce-scatter.2
  2787.1 464.8 all-reduce.180
